TPU v7x, 32 devices: a whole 2x2x4 slice. The times are simulated.
32 devices in a mesh: tm: 4 (over y, core), head: 2 (over x), branch: 4 (over z).
Axes of the slice: x: 2, y: 2, z: 4, core: 2. Of those that a mesh axis runs over, the one named last changes fastest.
Arguments:
- queries: bfloat16 [4, 4, 512, 20, 128], P('branch', 'tm', 'head'), may hold values from -8 to 8
- keys: bfloat16 [4, 4, 512, 20, 128], P('branch', 'tm', 'head'), may hold values from -5 to 5
- values: bfloat16 [4, 4, 512, 20, 128], P('branch', 'tm', 'head'), may hold values from -6 to 6
- ctx_keys: bfloat16 [4, 512, 20, 128], P('tm', ('head', 'branch')), may hold values from -5 to 5
- ctx_values: bfloat16 [4, 512, 20, 128], P('tm', ('head', 'branch')), may hold values from -6 to 6
- hidden: bfloat16 [4, 4, 512, 5120], P('branch', 'tm', 'head'), may hold values from -6 to 6
- out_weight: bfloat16 [2560, 5120], P('head'), may hold values from -0.5 to 0.5
- gates: float32 [16, 5120], replicated, may hold values from 0.5 to 2
- levels: int32 [4], replicated, may hold values from 0 to 15
- span_mask: int32 [4, 4], replicated, may hold values from 0 to 1, as said below
- prefix: int32 [1], replicated, may hold values from 1 to 3
Outputs:
- updated: bfloat16 [4, 4, 512, 5120], P('branch', 'tm', 'head')
Inputs may be any that keep to these rules, and one draw needn't show every extreme that they name: `span_mask`: 1 on the diagonal and in the first column, 0 above the diagonal.
All inputs are finite; a program needn't handle non-finite values.
Results may differ from a plain program's by a relative error of at most 0.01.
Values may be sent and summed in bfloat16 or wider, within the bound.
No kernel may reach another device: no remote copies, remote signals or barrier semaphores. Data moves between devices by JAX's collectives and lax.ppermute only.
A program may use at most 256 MiB of HBM per device.

v0:
```python
import math
import jax
import jax.numpy as jnp
from jax import lax
from jax.sharding import PartitionSpec as P

NEG_BIG = -1e30


def fold_block(running, key_block, heads_q, mask_row, score_scale):
    run_max, run_total, run_acc = running
    block_keys = key_block[0]
    block_values = key_block[1]
    row_count = block_keys.shape[0]
    span_len = heads_q.shape[0]
    row_span = jnp.arange(row_count, dtype=jnp.int32) // span_len
    span_hits = row_span[:, None] == jnp.arange(mask_row.shape[0], dtype=jnp.int32)[None, :]
    visible = jnp.sum(jnp.where(span_hits, mask_row[None, :], 0), axis=1) > 0
    scores = (
        jnp.einsum("qhd,khd->hqk", heads_q, block_keys, preferred_element_type=jnp.float32)
        * score_scale
    )
    block_max = jnp.max(jnp.where(visible[None, None, :], scores, NEG_BIG), axis=2)
    new_max = jnp.maximum(run_max, block_max)
    weights = jnp.where(visible[None, None, :], jnp.exp(scores - new_max[:, :, None]), 0.0)
    new_total = jnp.sum(weights, axis=2)
    new_acc = jnp.einsum(
        "hqk,khd->hqd",
        weights.astype(jnp.bfloat16),
        block_values,
        preferred_element_type=jnp.float32,
    )
    return (new_max, new_total, new_acc)


def body(
    queries,
    keys,
    values,
    ctx_keys,
    ctx_values,
    hidden,
    out_weight,
    gates,
    levels,
    span_mask,
    prefix,
):
    span_index = lax.axis_index("tm")
    heads_q, heads_k, heads_v = (
        lax.all_to_all(queries[0, 0], "head", split_axis=1, concat_axis=0, tiled=True),
        lax.all_to_all(keys[0, 0], "head", split_axis=1, concat_axis=0, tiled=True),
        lax.all_to_all(values[0, 0], "head", split_axis=1, concat_axis=0, tiled=True),
    )
    split_parts = (
        lax.all_to_all(ctx_keys[0], "head", split_axis=1, concat_axis=0, tiled=True),
        lax.all_to_all(ctx_values[0], "head", split_axis=1, concat_axis=0, tiled=True),
    )
    ctx_full_k, ctx_full_v = (
        lax.all_gather(split_parts[0], "branch", axis=0, tiled=True),
        lax.all_gather(split_parts[1], "branch", axis=0, tiled=True),
    )
    use_context = span_index < prefix[0]
    slot_kv = jnp.where(
        use_context, jnp.stack([ctx_full_k, ctx_full_v]), jnp.stack([heads_k, heads_v])
    )
    span_len = heads_q.shape[0]
    group_heads = heads_q.shape[1]
    head_dim = heads_q.shape[2]
    score_scale = 1.0 / math.sqrt(head_dim)
    mask_row = lax.dynamic_index_in_dim(span_mask, span_index, 0, keepdims=False)
    initial = (
        jnp.full((group_heads, span_len), NEG_BIG, jnp.float32),
        jnp.zeros((group_heads, span_len), jnp.float32),
        jnp.zeros((group_heads, span_len, head_dim), jnp.float32),
    )
    run_max, run_total, run_acc = fold_block(
        initial, lax.all_gather(slot_kv, "tm", axis=1, tiled=True), heads_q, mask_row, score_scale
    )
    attended = (run_acc / run_total[:, :, None]).astype(jnp.bfloat16)
    weight_heads = out_weight.reshape(group_heads, head_dim, out_weight.shape[1])
    projected = lax.psum_scatter(
        jnp.einsum(
            "hqd,hdn->qn", attended, weight_heads, preferred_element_type=jnp.float32
        ).astype(jnp.bfloat16),
        "head",
        scatter_dimension=0,
        tiled=True,
    ).astype(jnp.float32)
    level_now = lax.dynamic_index_in_dim(levels, span_index, 0, keepdims=False)
    gate_row = lax.dynamic_index_in_dim(gates, level_now, 0, keepdims=False)
    mixed_rows = hidden[0, 0].astype(jnp.float32) + gate_row[None, :] * projected
    return mixed_rows.astype(jnp.bfloat16)[None, None]


def solution(mesh):
    return jax.shard_map(
        body,
        mesh=mesh,
        in_specs=(
            P("branch", "tm", "head", None, None),
            P("branch", "tm", "head", None, None),
            P("branch", "tm", "head", None, None),
            P("tm", ("head", "branch"), None, None),
            P("tm", ("head", "branch"), None, None),
            P("branch", "tm", "head", None),
            P("head", None),
            P(),
            P(),
            P(),
            P(),
        ),
        out_specs=P("branch", "tm", "head", None),
        check_vma=False,
    )
```

profile of v0, /device:TPU:0, one launch (start us, length us, event | category | flops | bytes accessed | tf_op | source)
XLA Modules:
  0.0 301.1 jit_solution(17909818051579816194)
XLA Ops:
  6.5 0.0 copy-start
  6.5 0.0 all-gather.6.cloned.1.call-start
  6.5 10.9 %all_to_all.84 = bf16[64,20,128]{2,0,1:T(8,128)(2,1)S(1)} all-to-all(bf16[64,20,128]{2,0,1:T(8,128)(2,1)} %bitcast.86), channel_id=1, replica_groups=mesh['tm'=4,'head'=2,'branch'=4] {'head'}, dimensions={1} | all-to-all | bytes 655360 | tf_op jit(solution)/shard_map/all_to_all | solution.py:57
  17.5 0.7 copy.18
  18.2 0.0 all-gather.6.cloned.1.call-update
  18.3 0.0 all-gather.4.cloned.1.call-start
  18.3 9.0 %all_to_all.85 = bf16[64,20,128]{2,0,1:T(8,128)(2,1)S(1)} all-to-all(bf16[64,20,128]{2,0,1:T(8,128)(2,1)} %bitcast.87), channel_id=1, replica_groups=mesh['tm'=4,'head'=2,'branch'=4] {'head'}, dimensions={1} | all-to-all | bytes 655360 | tf_op jit(solution)/shard_map/all_to_all | solution.py:56
  27.3 0.7 copy.17
  28.1 0.0 all-gather.4.cloned.1.call-update
  28.1 18.9 %all_to_all.86 = bf16[256,20,128]{2,0,1:T(8,128)(2,1)S(1)} all-to-all(bf16[256,20,128]{2,0,1:T(8,128)(2,1)} %bitcast.77), channel_id=1, replica_groups=mesh['tm'=4,'head'=2,'branch'=4] {'head'}, dimensions={1} | all-to-all | bytes 2621440 | tf_op jit(solution)/shard_map/all_to_all | solution.py:52
  47.0 3.6 %all-to-all-start.3 = ((bf16[256,20,128]{2,0,1:T(8,128)(2,1)}), bf16[256,20,128]{2,0,1:T(8,128)(2,1)S(1)}, u32[]{:S(2)}, u32[]{:S(2)}) async-start(bf16[256,20,128]{2,0,1:T(8,128)(2,1)} %bitcast.78), calls=%async_computation.3 | async-start | bytes 2621440 | tf_op jit(solution)/shard_map/all_to_all | solution.py:53
  50.6 0.0 all-gather.8.cloned.1.call-start
  51.3 1.2 copy.19
  52.5 12.6 %all-to-all-done.3 = bf16[256,20,128]{2,0,1:T(8,128)(2,1)S(1)} async-done(((bf16[256,20,128]{2,0,1:T(8,128)(2,1)}), bf16[256,20,128]{2,0,1:T(8,128)(2,1)S(1)}, u32[]{:S(2)}, u32[]{:S(2)}) %all-to-all-start.3) | async-done | bytes 1310752 | tf_op jit(solution)/shard_map/all_to_all | solution.py:53
  65.1 0.1 copy.20
  65.2 0.0 all-gather.6.cloned.1.call-done
  65.2 19.5 %all-gather.4.cloned.1.call-done = bf16[512,10,128]{2,0,1:T(8,128)(2,1)} async-done(((bf16[128,10,128]{2,0,1:T(8,128)(2,1)}), bf16[512,10,128]{2,0,1:T(8,128)(2,1)}) %all-gather.4.cloned.1.call-update) | async-done | bytes 1310736 | tf_op jit(solution)/shard_map/all_gather | solution.py:60
  84.7 3.4 %maximum_select_fusion = bf16[2,512,10,128]{3,1,2,0:T(8,128)(2,1)} fusion(bf16[1,512,10,128]{3,1,2,0:T(8,128)(2,1)} %bitcast.84, bf16[1,512,10,128]{3,1,2,0:T(8,128)(2,1)} %bitcast.85, bf16[1,512,10,128]{3,1,2,0:T(8,128)(2,1)S(1)} %bitcast.76, bf16[1,512,10,128]{3,1,2,0:T(8,128)(2,1)} %bitcast.75, pred[]{:T(512)S(6)} %lt.15), kind=kLoop, calls=%fused_computation.13 | loop fusion | flops 3932160 | bytes 7864321 | tf_op jit(solution)/shard_map/jit(_where)/select_n | solution.py:64
  88.1 0.0 all-gather.8.cloned.1.call-update
  88.1 3.6 %all-to-all-start.4 = ((bf16[256,20,128]{2,0,1:T(8,128)(2,1)}), bf16[256,20,128]{2,0,1:T(8,128)(2,1)S(1)}, u32[]{:S(2)}, u32[]{:S(2)}) async-start(bf16[256,20,128]{2,0,1:T(8,128)(2,1)} %bitcast.24), calls=%async_computation.4 | async-start | bytes 2621440 | tf_op jit(solution)/shard_map/all_to_all | solution.py:51
  91.8 0.0 reduce-scatter.2.cloned.1.call-start
  91.8 0.7 dynamic-slice_bitcast_fusion
  92.5 0.1 select_reduce_fusion.1
  92.6 15.1 %all-to-all-done.4 = bf16[256,20,128]{2,0,1:T(8,128)(2,1)S(1)} async-done(((bf16[256,20,128]{2,0,1:T(8,128)(2,1)}), bf16[256,20,128]{2,0,1:T(8,128)(2,1)S(1)}, u32[]{:S(2)}, u32[]{:S(2)}) %all-to-all-start.4) | async-done | bytes 1310752 | tf_op jit(solution)/shard_map/all_to_all | solution.py:51
  107.7 0.1 copy.21
  107.8 49.7 %all-gather.8.cloned.1.call-done = bf16[2,2048,10,128]{3,1,2,0:T(8,128)(2,1)} async-done(((bf16[2,512,10,128]{3,1,2,0:T(8,128)(2,1)}), bf16[2,2048,10,128]{3,1,2,0:T(8,128)(2,1)}) %all-gather.8.cloned.1.call-update) | async-done | bytes 10485776 | tf_op jit(solution)/shard_map/all_gather | solution.py:78
  157.5 18.1 %select_reduce_fusion = (f32[10,512]{1,0:T(8,128)S(1)}, f32[10,2048,512]{2,1,0:T(8,128)}) fusion(pred[2048]{0:T(1024)(128)(4,1)S(1)} %broadcast_compare_fusion, bf16[512,10,128]{2,0,1:T(8,128)(2,1)S(1)} %bitcast.79, bf16[2,2048,10,128]{3,1,2,0:T(8,128)(2,1)} %all-gather.8.cloned.1.call-done), kind=kOutput, calls=%fused_computation.3 | convolution fusion | flops 2715806720 | bytes 48519168 | tf_op jit(solution)/shard_map/qhd,khd->hqk/dot_general | solution.py:20
  175.6 17.4 %bitcast_reduce_fusion = f32[10,512]{1,0:T(8,128)S(1)} fusion(f32[10,2048,512]{2,1,0:T(8,128)} %get-tuple-element.6, f32[10,512]{1,0:T(8,128)S(1)} %broadcast_maximum_fusion, pred[2048]{0:T(1024)(128)(4,1)S(1)} %broadcast_compare_fusion), kind=kLoop, calls=%fused_computation | loop fusion | flops 41937920 | bytes 41986048 | tf_op jit(solution)/shard_map/reduce_sum | solution.py:26
  193.1 19.8 %divide_convert_fusion.4 = bf16[10,512,128]{2,1,0:T(8,128)(2,1)S(1)} fusion(bf16[2,2048,10,128]{3,1,2,0:T(8,128)(2,1)} %all-gather.8.cloned.1.call-done, f32[10,2048,512]{2,1,0:T(8,128)} %get-tuple-element.6, f32[10,512]{1,0:T(8,128)S(1)} %broadcast_maximum_fusion, pred[2048]{0:T(1024)(128)(4,1)S(1)} %broadcast_compare_fusion, ...), kind=kOutput, calls=%fused_computation.14.clone.clone.1 | convolution fusion | flops 2727608320 | bytes 48539648 | tf_op jit(solution)/shard_map/hqk,khd->hqd/dot_general | solution.py:27
  212.9 11.5 %bitcast_convert_fusion.2 = bf16[512,5120]{1,0:T(8,128)(2,1)} fusion(bf16[10,128,5120]{2,1,0:T(8,128)(2,1)} %bitcast.89, bf16[10,512,128]{2,1,0:T(8,128)(2,1)S(1)} %divide_convert_fusion.4), kind=kOutput, calls=%fused_computation.6 | convolution fusion | flops 6713507840 | bytes 19660800 | tf_op jit(solution)/shard_map/hqd,hdn->qn/dot_general | solution.py:83
  224.4 0.0 copy-start.2
  224.4 0.0 copy-start.1
  224.4 0.0 reduce-scatter.2.cloned.1.call-update
  224.4 0.6 copy-done.2
  225.1 0.6 dynamic_slice.12
  227.6 0.0 copy-done
  227.6 62.7 %reduce-scatter.2.cloned.1.call-done = bf16[256,5120]{1,0:T(8,128)(2,1)} async-done(((bf16[512,5120]{1,0:T(8,128)(2,1)}), bf16[256,5120]{1,0:T(8,128)(2,1)}) %reduce-scatter.2.cloned.1.call-update) | async-done | bytes 2621456 | tf_op jit(solution)/shard_map/reduce_scatter | solution.py:82
  290.4 0.0 copy-done.1
  290.4 4.2 %fusion.4 = bf16[1,1,256,5120]{3,2,1,0:T(8,128)(2,1)} fusion(bf16[256,5120]{1,0:T(8,128)(2,1)} %reduce-scatter.2.cloned.1.call-done, bf16[1,1,256,5120]{3,2,1,0:T(8,128)(2,1)S(1)} %copy-done.1, f32[5120]{0:T(1024)S(1)} %bitcast.88), kind=kLoop, calls=%fused_computation.12 | loop fusion | flops 6553600 | bytes 7884800 | tf_op jit(solution)/shard_map/broadcast_in_dim | solution.py:93
  (4 shorter events, 0.0 us)
Async XLA Ops:
  6.5 221.1 %copy-start = (f32[16,5120]{1,0:T(8,128)S(1)}, f32[16,5120]{1,0:T(8,128)}, u32[]{:S(2)}) copy-start(f32[16,5120]{1,0:T(8,128)} %param.18) | copy-start | bytes 983044
  6.5 58.7 %all-gather.6.cloned.1.call-start = ((), (), s32[]{:S(2)}) async-start(), calls=%async_computation.7 | async-start | bytes 1638400 | tf_op jit(solution)/shard_map/all_gather | solution.py:61
  18.3 66.5 %all-gather.4.cloned.1.call-start = ((), (), s32[]{:S(2)}) async-start(), calls=%async_computation.6 | async-start | bytes 1638400 | tf_op jit(solution)/shard_map/all_gather | solution.py:60
  47.0 18.1 %all-to-all-start.3 = ((bf16[256,20,128]{2,0,1:T(8,128)(2,1)}), bf16[256,20,128]{2,0,1:T(8,128)(2,1)S(1)}, u32[]{:S(2)}, u32[]{:S(2)}) async-start(bf16[256,20,128]{2,0,1:T(8,128)(2,1)} %bitcast.78), calls=%async_computation.3 | async-start | bytes 2621440 | tf_op jit(solution)/shard_map/all_to_all | solution.py:53
  50.6 106.9 %all-gather.8.cloned.1.call-start = ((), (), s32[]{:S(2)}) async-start(), calls=%async_computation.8 | async-start | bytes 13107200 | tf_op jit(solution)/shard_map/all_gather | solution.py:78
  88.1 19.6 %all-to-all-start.4 = ((bf16[256,20,128]{2,0,1:T(8,128)(2,1)}), bf16[256,20,128]{2,0,1:T(8,128)(2,1)S(1)}, u32[]{:S(2)}, u32[]{:S(2)}) async-start(bf16[256,20,128]{2,0,1:T(8,128)(2,1)} %bitcast.24), calls=%async_computation.4 | async-start | bytes 2621440 | tf_op jit(solution)/shard_map/all_to_all | solution.py:51
  91.8 198.6 %reduce-scatter.2.cloned.1.call-start = ((), (), s32[]{:S(2)}) async-start(), calls=%async_computation.9 | async-start | bytes 7864320 | tf_op jit(solution)/shard_map/reduce_scatter | solution.py:82
  224.4 0.7 copy-start.2
  224.4 66.0 %copy-start.1 = (bf16[1,1,256,5120]{3,2,1,0:T(8,128)(2,1)S(1)}, bf16[1,1,256,5120]{3,2,1,0:T(8,128)(2,1)}, u32[]{:S(2)}) copy-start(bf16[1,1,256,5120]{3,2,1,0:T(8,128)(2,1)} %param.16) | copy-start | bytes 7864324
Sparse Core Ops, SparseCore 0:
  18.4 33.1 all-gather.5
  53.1 31.5 all-gather.3
  88.2 69.2 all-gather.7
  224.6 65.7 reduce-scatter.1
where the time goes:
time: 302 us; the launch traced here: 301 us
  waiting for transfers between devices  160 us (53%)
  matrix products  49.4 us (16%)
  blocking collectives  38.8 us (13%)
  other arithmetic  25.1 us (8%)
  between operations  15.8 us (5%)
  starting transfers between devices  7.39 us (2%)
  local copies, waits for them, and re-layouts  4.8 us (2%)
    reduce_scatter x1, waiting for transfers between devices, body(): lax.psum_scatter(jnp.einsum('hqd,hdn->qn', attended, weight_heads, prefer...  62.7 us
    all_gather x1, waiting for transfers between devices, body(): lax.all_gather(slot_kv, 'tm', axis=1, tiled=True)  49.7 us
    dot_general x1, matrix products, fold_block(): jnp.einsum('hqk,khd->hqd', weights.astype(jnp.bfloat16), block_values, pr...  19.8 us
    all_gather x1, waiting for transfers between devices, body(): lax.all_gather(split_parts[0], 'branch', axis=0, tiled=True)  19.5 us
    all_to_all x1, blocking collectives, body(): lax.all_to_all(keys[0, 0], 'head', split_axis=1, concat_axis=0, tiled=True)  18.9 us
    dot_general x1, matrix products, fold_block(): jnp.einsum('qhd,khd->hqk', heads_q, block_keys, preferred_element_type=jn...  18.1 us
    reduce_sum x1, other arithmetic, fold_block(): new_total = jnp.sum(weights, axis=2)  17.4 us
    all_to_all x1, waiting for transfers between devices, body(): lax.all_to_all(queries[0, 0], 'head', split_axis=1, concat_axis=0, tiled=...  15.1 us
  transfers between devices with their start and end apart: 6, of which 5 were waited for; matrix products, arithmetic and copies ran while one was open for 1% of the time, Pallas kernels for 0%

commit v1 on v0

--- a/solution.py
+++ b/solution.py
@@ -5,6 +5,25 @@
 from jax.sharding import PartitionSpec as P
 
 NEG_BIG = -1e30
+
+
+def gather_around(shard, axis, dim):
+    size, here, rows = (lax.axis_size(axis), lax.axis_index(axis), shard.shape[dim])
+    forward = [(i, (i + 1) % size) for i in range(size)]
+    left = [(i, (i - 1) % size) for i in range(size)]
+    out = jnp.zeros((*shard.shape[:dim], size * rows, *shard.shape[dim + 1 :]), shard.dtype)
+    out = lax.dynamic_update_slice_in_dim(out, shard, here * rows, axis=dim)
+    from_left = from_right = shard
+    halfway = size // 2
+    for turn in range(1, halfway + 1):
+        from_left = lax.ppermute(from_left, axis, forward)
+        out = lax.dynamic_update_slice_in_dim(out, from_left, (here - turn) % size * rows, axis=dim)
+        if turn < size - halfway:
+            from_right = lax.ppermute(from_right, axis, left)
+            out = lax.dynamic_update_slice_in_dim(
+                out, from_right, (here + turn) % size * rows, axis=dim
+            )
+    return out
 
 
 def fold_block(running, key_block, heads_q, mask_row, score_scale):
@@ -57,7 +76,7 @@
         lax.all_to_all(ctx_values[0], "head", split_axis=1, concat_axis=0, tiled=True),
     )
     ctx_full_k, ctx_full_v = (
-        lax.all_gather(split_parts[0], "branch", axis=0, tiled=True),
+        gather_around(split_parts[0], "branch", 0),
         lax.all_gather(split_parts[1], "branch", axis=0, tiled=True),
     )
     use_context = span_index < prefix[0]

time: 302 us -> 291 us (0.964)
  blocking collectives: 38.8 us -> 20 us
  starting transfers between devices: 7.39 us -> 16.1 us
  waiting for transfers between devices: 160 us -> 153 us
  local copies, waits for them, and re-layouts: 4.8 us -> 11.5 us
    all_gather x1 -> x0, waiting for transfers between devices: 19.5 us -> none  [body(): lax.all_gather(split_parts[0], 'branch', axis=0, tiled=True)]
    all_to_all x1 -> x0, blocking collectives: 18.9 us -> none  [body(): lax.all_to_all(keys[0, 0], 'head', split_axis=1, concat_axis=0, tiled=True)]
    all_to_all x0 -> x1, waiting for transfers between devices: none -> 13.4 us  [body(): lax.all_to_all(keys[0, 0], 'head', split_axis=1, concat_axis=0, tiled=True)]
    all_to_all x1, waiting for transfers between devices: 12.6 us -> 0.01 us  [body(): lax.all_to_all(values[0, 0], 'head', split_axis=1, concat_axis=0, tiled=T...]
    ppermute x0 -> x3, waiting for transfers between devices: none -> 12.5 us  [the longest x1 6.64 us: gather_around(): from_right = lax.ppermute(from_right, axis, left)]
    dynamic_update_slice x0 -> x4, local copies, waits for them, and re-layouts: none -> 5.14 us  [the longest x2 3.57 us: gather_around(): lax.dynamic_update_slice_in_dim(out, from_left, (here - turn) % size * ro...]
    ppermute x0 -> x3, starting transfers between devices: none -> 5.12 us  [the longest x1 3.29 us: gather_around(): from_right = lax.ppermute(from_right, axis, left)]
    all_to_all x0 -> x1, starting transfers between devices: none -> 3.63 us  [body(): lax.all_to_all(keys[0, 0], 'head', split_axis=1, concat_axis=0, tiled=True)]
  transfers between devices with their start and end apart: 6 -> 9, of which waited for: 5 -> 6; matrix products, arithmetic and copies ran while one was open for 1% -> 4% of each run, Pallas kernels for 0% -> 0%
where the time goes in v1:
time: 291 us
  waiting for transfers between devices  153 us (53%)
  matrix products  49.4 us (17%)
  other arithmetic  25.1 us (9%)
  blocking collectives  20 us (7%)
  starting transfers between devices  16.1 us (6%)
  between operations  15.9 us (5%)
  local copies, waits for them, and re-layouts  11.5 us (4%)
    reduce_scatter x1, waiting for transfers between devices, body(): lax.psum_scatter(jnp.einsum('hqd,hdn->qn', attended, weight_heads, prefer...  62.7 us
    all_gather x1, waiting for transfers between devices, body(): lax.all_gather(slot_kv, 'tm', axis=1, tiled=True)  49 us
    dot_general x1, matrix products, fold_block(): jnp.einsum('hqk,khd->hqd', weights.astype(jnp.bfloat16), block_values, pr...  19.9 us
    dot_general x1, matrix products, fold_block(): jnp.einsum('qhd,khd->hqk', heads_q, block_keys, preferred_element_type=jn...  18.1 us
    reduce_sum x1, other arithmetic, fold_block(): new_total = jnp.sum(weights, axis=2)  17.4 us
    all_to_all x1, waiting for transfers between devices, body(): lax.all_to_all(queries[0, 0], 'head', split_axis=1, concat_axis=0, tiled=...  14.8 us
    all_to_all x1, waiting for transfers between devices, body(): lax.all_to_all(keys[0, 0], 'head', split_axis=1, concat_axis=0, tiled=True)  13.4 us
    dot_general x1, matrix products, body(): jnp.einsum('hqd,hdn->qn', attended, weight_heads, preferred_element_type=...  11.5 us
  transfers between devices with their start and end apart: 9, of which 6 were waited for; matrix products, arithmetic and copies ran while one was open for 4% of the time, Pallas kernels for 0%

profile of v1, /device:TPU:0, one launch (start us, length us, event | category | flops | bytes accessed | tf_op | source)
XLA Modules:
  0.0 290.5 jit_solution(10859154314464583453)
XLA Ops:
  6.5 0.0 copy-start
  6.5 0.0 all-gather.3.cloned.1.call-start
  6.5 10.9 %all_to_all.84 = bf16[64,20,128]{2,0,1:T(8,128)(2,1)S(1)} all-to-all(bf16[64,20,128]{2,0,1:T(8,128)(2,1)} %bitcast.94), channel_id=1, replica_groups=mesh['tm'=4,'head'=2,'branch'=4] {'head'}, dimensions={1} | all-to-all | bytes 655360 | tf_op jit(solution)/shard_map/all_to_all | solution.py:76
  17.5 0.7 copy.18
  18.2 0.0 all-gather.3.cloned.1.call-update
  18.2 9.0 %all_to_all.85 = bf16[64,20,128]{2,0,1:T(8,128)(2,1)S(1)} all-to-all(bf16[64,20,128]{2,0,1:T(8,128)(2,1)} %bitcast.95), channel_id=1, replica_groups=mesh['tm'=4,'head'=2,'branch'=4] {'head'}, dimensions={1} | all-to-all | bytes 655360 | tf_op jit(solution)/shard_map/all_to_all | solution.py:75
  27.3 3.6 %all-to-all-start.2 = ((bf16[256,20,128]{2,0,1:T(8,128)(2,1)}), bf16[256,20,128]{2,0,1:T(8,128)(2,1)S(1)}, u32[]{:S(2)}, u32[]{:S(2)}) async-start(bf16[256,20,128]{2,0,1:T(8,128)(2,1)} %bitcast.84), calls=%async_computation.2 | async-start | bytes 2621440 | tf_op jit(solution)/shard_map/all_to_all | solution.py:71
  30.9 1.8 collective-permute-start
  32.8 13.4 %all-to-all-done.2 = bf16[256,20,128]{2,0,1:T(8,128)(2,1)S(1)} async-done(((bf16[256,20,128]{2,0,1:T(8,128)(2,1)}), bf16[256,20,128]{2,0,1:T(8,128)(2,1)S(1)}, u32[]{:S(2)}, u32[]{:S(2)}) %all-to-all-start.2) | async-done | bytes 1310752 | tf_op jit(solution)/shard_map/all_to_all | solution.py:71
  46.1 3.6 %all-to-all-start.3 = ((bf16[256,20,128]{2,0,1:T(8,128)(2,1)}), bf16[256,20,128]{2,0,1:T(8,128)(2,1)S(1)}, u32[]{:S(2)}, u32[]{:S(2)}) async-start(bf16[256,20,128]{2,0,1:T(8,128)(2,1)} %bitcast.85), calls=%async_computation.3 | async-start | bytes 2621440 | tf_op jit(solution)/shard_map/all_to_all | solution.py:72
  49.8 0.0 all-gather.5.cloned.1.call-start
  50.5 3.3 %collective-permute-start.1 = (bf16[128,10,128]{2,0,1:T(8,128)(2,1)S(1)}, bf16[128,10,128]{2,0,1:T(8,128)(2,1)S(1)}, u32[]{:S(2)}, u32[]{:S(2)}) collective-permute-start(bf16[128,10,128]{2,0,1:T(8,128)(2,1)S(1)} %bitcast.89), channel_id=1, source_target_pairs={{0,3},{1,0},{2,1},{3,2},{4,7},{5,4},{6,5},{7,6},{8,11},{9,8},{10,9... | collective-permute-start | bytes 983048 | tf_op jit(solution)/shard_map/ppermute | solution.py:22
  53.8 1.3 stack.26
  55.1 0.8 constant_dynamic-update-slice_fusion
  55.9 0.0 collective-permute-done
  55.9 0.0 collective-permute-start.2
  55.9 1.8 bitcast_dynamic-update-slice_fusion.2
  57.7 6.6 %collective-permute-done.1 = bf16[128,10,128]{2,0,1:T(8,128)(2,1)S(1)} collective-permute-done((bf16[128,10,128]{2,0,1:T(8,128)(2,1)S(1)}, bf16[128,10,128]{2,0,1:T(8,128)(2,1)S(1)}, u32[]{:S(2)}, u32[]{:S(2)}) %collective-permute-start.1) | collective-permute-done | bytes 327712 | tf_op jit(solution)/shard_map/ppermute | solution.py:22
  64.3 0.8 bitcast_dynamic-update-slice_fusion.1
  65.1 1.1 copy.19
  66.2 0.0 copy-start.1
  66.2 0.0 all-to-all-done.3
  66.2 1.1 copy.20
  67.4 5.9 %collective-permute-done.2 = bf16[128,10,128]{2,0,1:T(8,128)(2,1)} collective-permute-done((bf16[128,10,128]{2,0,1:T(8,128)(2,1)}, bf16[128,10,128]{2,0,1:T(8,128)(2,1)}, u32[]{:S(2)}, u32[]{:S(2)}) %collective-permute-start.2) | collective-permute-done | bytes 327712 | tf_op jit(solution)/shard_map/ppermute | solution.py:19
  73.3 1.8 bitcast_dynamic-update-slice_fusion
  75.0 0.0 all-gather.3.cloned.1.call-done
  75.0 0.0 copy-done.1
  75.0 3.4 %maximum_select_fusion = bf16[2,512,10,128]{3,1,2,0:T(8,128)(2,1)} fusion(bf16[1,512,10,128]{3,1,2,0:T(8,128)(2,1)} %bitcast.93, bf16[1,512,10,128]{3,1,2,0:T(8,128)(2,1)} %bitcast_dynamic-update-slice_fusion, bf16[1,512,10,128]{3,1,2,0:T(8,128)(2,1)} %bitcast.83, bf16[1,512,10,128]{3,1,2,0:T(8,128)(2,1)S(1)} %bitcast.82, pred[]{:T(512)S(6)} %lt.41), kind=kLoop, calls=%fused_computation.13 | loop fusion | flops 3932160 | bytes 7864321 | tf_op jit(solution)/shard_map/jit(_where)/select_n | solution.py:83
  78.4 0.0 all-gather.5.cloned.1.call-update
  78.4 3.6 %all-to-all-start.4 = ((bf16[256,20,128]{2,0,1:T(8,128)(2,1)}), bf16[256,20,128]{2,0,1:T(8,128)(2,1)S(1)}, u32[]{:S(2)}, u32[]{:S(2)}) async-start(bf16[256,20,128]{2,0,1:T(8,128)(2,1)} %bitcast.28), calls=%async_computation.4 | async-start | bytes 2621440 | tf_op jit(solution)/shard_map/all_to_all | solution.py:70
  82.1 0.0 reduce-scatter.2.cloned.1.call-start
  82.1 0.7 fusion.9
  82.8 0.1 select_reduce_fusion.1
  82.9 14.8 %all-to-all-done.4 = bf16[256,20,128]{2,0,1:T(8,128)(2,1)S(1)} async-done(((bf16[256,20,128]{2,0,1:T(8,128)(2,1)}), bf16[256,20,128]{2,0,1:T(8,128)(2,1)S(1)}, u32[]{:S(2)}, u32[]{:S(2)}) %all-to-all-start.4) | async-done | bytes 1310752 | tf_op jit(solution)/shard_map/all_to_all | solution.py:70
  97.8 0.1 copy.21
  97.9 49.0 %all-gather.5.cloned.1.call-done = bf16[2,2048,10,128]{3,1,2,0:T(8,128)(2,1)} async-done(((bf16[2,512,10,128]{3,1,2,0:T(8,128)(2,1)}), bf16[2,2048,10,128]{3,1,2,0:T(8,128)(2,1)}) %all-gather.5.cloned.1.call-update) | async-done | bytes 10485776 | tf_op jit(solution)/shard_map/all_gather | solution.py:97
  146.9 18.1 %select_reduce_fusion = (f32[10,512]{1,0:T(8,128)S(1)}, f32[10,2048,512]{2,1,0:T(8,128)}) fusion(pred[2048]{0:T(1024)(128)(4,1)S(1)} %broadcast_compare_fusion, bf16[512,10,128]{2,0,1:T(8,128)(2,1)S(1)} %bitcast.86, bf16[2,2048,10,128]{3,1,2,0:T(8,128)(2,1)} %all-gather.5.cloned.1.call-done), kind=kOutput, calls=%fused_computation.3 | convolution fusion | flops 2715806720 | bytes 48519168 | tf_op jit(solution)/shard_map/qhd,khd->hqk/dot_general | solution.py:39
  165.0 17.4 %bitcast_reduce_fusion = f32[10,512]{1,0:T(8,128)S(1)} fusion(f32[10,2048,512]{2,1,0:T(8,128)} %get-tuple-element.6, f32[10,512]{1,0:T(8,128)S(1)} %broadcast_maximum_fusion, pred[2048]{0:T(1024)(128)(4,1)S(1)} %broadcast_compare_fusion), kind=kLoop, calls=%fused_computation | loop fusion | flops 41937920 | bytes 41986048 | tf_op jit(solution)/shard_map/reduce_sum | solution.py:45
  182.4 19.9 %divide_convert_fusion.4 = bf16[10,512,128]{2,1,0:T(8,128)(2,1)S(1)} fusion(bf16[2,2048,10,128]{3,1,2,0:T(8,128)(2,1)} %all-gather.5.cloned.1.call-done, f32[10,2048,512]{2,1,0:T(8,128)} %get-tuple-element.6, f32[10,512]{1,0:T(8,128)S(1)} %broadcast_maximum_fusion, pred[2048]{0:T(1024)(128)(4,1)S(1)} %broadcast_compare_fusion, ...), kind=kOutput, calls=%fused_computation.14.clone.clone.1 | convolution fusion | flops 2727608320 | bytes 48539648 | tf_op jit(solution)/shard_map/hqk,khd->hqd/dot_general | solution.py:46
  202.3 11.5 %bitcast_convert_fusion.2 = bf16[512,5120]{1,0:T(8,128)(2,1)} fusion(bf16[10,128,5120]{2,1,0:T(8,128)(2,1)} %bitcast.97, bf16[10,512,128]{2,1,0:T(8,128)(2,1)S(1)} %divide_convert_fusion.4), kind=kOutput, calls=%fused_computation.6 | convolution fusion | flops 6713507840 | bytes 19660800 | tf_op jit(solution)/shard_map/hqd,hdn->qn/dot_general | solution.py:102
  213.8 0.0 copy-start.3
  213.8 0.0 copy-start.2
  213.8 0.0 reduce-scatter.2.cloned.1.call-update
  213.8 0.6 copy-done.3
  214.5 0.6 dynamic_slice.12
  217.0 0.0 copy-done
  217.0 62.7 %reduce-scatter.2.cloned.1.call-done = bf16[256,5120]{1,0:T(8,128)(2,1)} async-done(((bf16[512,5120]{1,0:T(8,128)(2,1)}), bf16[256,5120]{1,0:T(8,128)(2,1)}) %reduce-scatter.2.cloned.1.call-update) | async-done | bytes 2621456 | tf_op jit(solution)/shard_map/reduce_scatter | solution.py:101
  279.8 0.0 copy-done.2
  279.8 4.2 %fusion.4 = bf16[1,1,256,5120]{3,2,1,0:T(8,128)(2,1)} fusion(bf16[256,5120]{1,0:T(8,128)(2,1)} %reduce-scatter.2.cloned.1.call-done, bf16[1,1,256,5120]{3,2,1,0:T(8,128)(2,1)S(1)} %copy-done.2, f32[5120]{0:T(1024)S(1)} %bitcast.96), kind=kLoop, calls=%fused_computation.12 | loop fusion | flops 6553600 | bytes 7884800 | tf_op jit(solution)/shard_map/broadcast_in_dim | solution.py:112
  (5 shorter events, 0.1 us)
Async XLA Ops:
  6.5 210.5 %copy-start = (f32[16,5120]{1,0:T(8,128)S(1)}, f32[16,5120]{1,0:T(8,128)}, u32[]{:S(2)}) copy-start(f32[16,5120]{1,0:T(8,128)} %param.18) | copy-start | bytes 983044
  6.5 68.5 %all-gather.3.cloned.1.call-start = ((), (), s32[]{:S(2)}) async-start(), calls=%async_computation.6 | async-start | bytes 1638400 | tf_op jit(solution)/shard_map/all_gather | solution.py:80
  27.3 18.9 %all-to-all-start.2 = ((bf16[256,20,128]{2,0,1:T(8,128)(2,1)}), bf16[256,20,128]{2,0,1:T(8,128)(2,1)S(1)}, u32[]{:S(2)}, u32[]{:S(2)}) async-start(bf16[256,20,128]{2,0,1:T(8,128)(2,1)} %bitcast.84), calls=%async_computation.2 | async-start | bytes 2621440 | tf_op jit(solution)/shard_map/all_to_all | solution.py:71
  30.9 24.9 %collective-permute-start = (bf16[128,10,128]{2,0,1:T(8,128)(2,1)S(1)}, bf16[128,10,128]{2,0,1:T(8,128)(2,1)}, u32[]{:S(2)}, u32[]{:S(2)}) collective-permute-start(bf16[128,10,128]{2,0,1:T(8,128)(2,1)S(1)} %bitcast.88), channel_id=1, source_target_pairs={{0,1},{1,2},{2,3},{3,0},{4,5},{5,6},{6,7},{7,4},{8,9},{9,10},{10,1... | collective-permute-start | bytes 983048 | tf_op jit(solution)/shard_map/ppermute | solution.py:19
  46.1 20.1 %all-to-all-start.3 = ((bf16[256,20,128]{2,0,1:T(8,128)(2,1)}), bf16[256,20,128]{2,0,1:T(8,128)(2,1)S(1)}, u32[]{:S(2)}, u32[]{:S(2)}) async-start(bf16[256,20,128]{2,0,1:T(8,128)(2,1)} %bitcast.85), calls=%async_computation.3 | async-start | bytes 2621440 | tf_op jit(solution)/shard_map/all_to_all | solution.py:72
  49.8 97.1 %all-gather.5.cloned.1.call-start = ((), (), s32[]{:S(2)}) async-start(), calls=%async_computation.7 | async-start | bytes 13107200 | tf_op jit(solution)/shard_map/all_gather | solution.py:97
  50.5 13.8 %collective-permute-start.1 = (bf16[128,10,128]{2,0,1:T(8,128)(2,1)S(1)}, bf16[128,10,128]{2,0,1:T(8,128)(2,1)S(1)}, u32[]{:S(2)}, u32[]{:S(2)}) collective-permute-start(bf16[128,10,128]{2,0,1:T(8,128)(2,1)S(1)} %bitcast.89), channel_id=1, source_target_pairs={{0,3},{1,0},{2,1},{3,2},{4,7},{5,4},{6,5},{7,6},{8,11},{9,8},{10,9... | collective-permute-start | bytes 983048 | tf_op jit(solution)/shard_map/ppermute | solution.py:22
  55.9 17.4 %collective-permute-start.2 = (bf16[128,10,128]{2,0,1:T(8,128)(2,1)}, bf16[128,10,128]{2,0,1:T(8,128)(2,1)}, u32[]{:S(2)}, u32[]{:S(2)}) collective-permute-start(bf16[128,10,128]{2,0,1:T(8,128)(2,1)} %collective-permute-done), channel_id=1, source_target_pairs={{0,1},{1,2},{2,3},{3,0},{4,5},{5,6},{6,7},{7,4},{8,9},{9,10},{10,1... | collective-permute-start | bytes 983048 | tf_op jit(solution)/shard_map/ppermute | solution.py:19
  66.2 8.8 %copy-start.1 = (bf16[256,2,10,128]{3,0,1,2:T(8,128)(2,1)S(1)}, bf16[256,2,10,128]{3,0,1,2:T(8,128)(2,1)}, u32[]{:S(2)}) copy-start(bf16[256,2,10,128]{3,0,1,2:T(8,128)(2,1)} %copy.19) | copy-start | bytes 3932164
  78.4 19.3 %all-to-all-start.4 = ((bf16[256,20,128]{2,0,1:T(8,128)(2,1)}), bf16[256,20,128]{2,0,1:T(8,128)(2,1)S(1)}, u32[]{:S(2)}, u32[]{:S(2)}) async-start(bf16[256,20,128]{2,0,1:T(8,128)(2,1)} %bitcast.28), calls=%async_computation.4 | async-start | bytes 2621440 | tf_op jit(solution)/shard_map/all_to_all | solution.py:70
  82.1 197.7 %reduce-scatter.2.cloned.1.call-start = ((), (), s32[]{:S(2)}) async-start(), calls=%async_computation.8 | async-start | bytes 7864320 | tf_op jit(solution)/shard_map/reduce_scatter | solution.py:101
  213.8 0.7 copy-start.3
  213.8 66.0 %copy-start.2 = (bf16[1,1,256,5120]{3,2,1,0:T(8,128)(2,1)S(1)}, bf16[1,1,256,5120]{3,2,1,0:T(8,128)(2,1)}, u32[]{:S(2)}) copy-start(bf16[1,1,256,5120]{3,2,1,0:T(8,128)(2,1)} %param.16) | copy-start | bytes 7864324
Sparse Core Ops, SparseCore 0:
  18.4 42.4 all-gather.2
  78.6 68.3 all-gather.4
  214.0 65.7 reduce-scatter.1
